TPU v7x, 512 devices: a whole 4x8x8 slice. The times are simulated.
512 devices in a mesh: row: 16 (over z, core), col: 32 (over x, y).
Axes of the slice: x: 4, y: 8, z: 8, core: 2. Of those that a mesh axis runs over, the one named last changes fastest.
Arguments:
- trail_adjoint: float32 [16384, 16384], P('row', 'col'), may hold values from -0.046875 to 0.046875
- panel: float32 [16384, 128], P('row', 'col')
- panel_adjoint: float32 [16384, 128], P('row', 'col'), may hold values from -6 to 6
- inv_diag: float32 [128, 128], replicated, as said below
- panel_index: int32 [1], replicated, may hold values from 832 to 895
Outputs:
- panel_grad: float32 [16384, 128], P('row', 'col')
- diag_grad: float32 [128, 128], P(None, 'col')
Inputs may be any that keep to these rules, and one draw needn't show every extreme that they name: inv_diag is lower triangular with a positive diagonal.
All inputs are finite; a program needn't handle non-finite values.
Results may differ from a plain program's by a relative error of at most 0.000075.
Values sent between devices are 32-bit elements; how exact they have to be, the bound alone decides.
No kernel may reach another device: no remote copies, remote signals or barrier semaphores. Data moves between devices by JAX's collectives and lax.ppermute only.
A program may use at most 64 MiB of HBM per device.

v0:
```python
import jax
import jax.numpy as jnp
from jax import lax
from jax.sharding import PartitionSpec as P


def broadcast(value, axis, root):
    mine = lax.axis_index(axis) == root
    return lax.psum(jnp.where(mine, value, jnp.zeros_like(value)), axis)


def body(trail_adjoint, panel, panel_adjoint, inv_diag, panel_index):
    rows_here, thin_cols = panel.shape
    panel_width = inv_diag.shape[0]
    ways_row = lax.axis_size("row")
    ways_col = lax.axis_size("col")
    ways_ratio = ways_col // ways_row
    col_here = lax.axis_index("col")
    index_k = panel_index[0]
    start_mod = jnp.mod(col_here - index_k - 1, ways_col)
    offset = start_mod // ways_row
    col_blocks = rows_here // (panel_width * ways_ratio)
    root_row = jnp.mod(col_here, ways_row)
    panel_rows = lax.all_gather(panel, "col", axis=1, tiled=True)
    shaped = broadcast(panel_rows, "row", root_row).reshape(
        col_blocks, ways_ratio, panel_width, panel_width
    )
    chosen = lax.dynamic_slice_in_dim(shaped, offset, 1, 1)
    column_panel = chosen.reshape(col_blocks * panel_width, panel_width)
    product = jnp.dot(
        trail_adjoint,
        column_panel,
        precision=lax.Precision.HIGHEST,
        preferred_element_type=jnp.float32,
    )
    placed = lax.dynamic_update_slice_in_dim(
        jnp.zeros((rows_here, panel_width), jnp.float32), panel_adjoint, col_here * thin_cols, 1
    )
    local_term = placed - 2.0 * product
    my_inverse = lax.dynamic_slice_in_dim(inv_diag, col_here * thin_cols, thin_cols, 1)
    contract_rows = (((0,), (0,)), ((), ()))
    thin_part = lax.psum_scatter(local_term, "col", scatter_dimension=1, tiled=True)
    full_rows = lax.all_gather(thin_part, "col", axis=1, tiled=True)
    panel_grad = jnp.dot(
        full_rows, my_inverse, precision=lax.Precision.HIGHEST, preferred_element_type=jnp.float32
    )
    gram_local = lax.dot_general(
        full_rows,
        panel,
        contract_rows,
        precision=lax.Precision.HIGHEST,
        preferred_element_type=jnp.float32,
    )
    gram_total = lax.psum(gram_local, "row")
    diag_grad = -lax.dot_general(
        inv_diag,
        gram_total,
        contract_rows,
        precision=lax.Precision.HIGHEST,
        preferred_element_type=jnp.float32,
    )
    return (panel_grad, diag_grad)


def solution(mesh):
    in_specs = (P("row", "col"), P("row", "col"), P("row", "col"), P(), P())
    out_specs = (P("row", "col"), P(None, "col"))
    return jax.shard_map(body, mesh=mesh, in_specs=in_specs, out_specs=out_specs, check_vma=False)
```

profile of v0, /device:TPU:1, one launch (start us, length us, event | category | flops | bytes accessed | tf_op | source)
XLA Modules:
  0.0 443.1 jit_solution(17022918917563937802)
XLA Ops:
  7.2 0.0 copy-start
  7.2 0.0 all-reduce.4.cloned.1.call-start
  7.2 40.0 %all-gather = f32[32,4,1024]{2,1,0:T(4,128)S(1)} all-gather(f32[1,4,1024]{2,1,0:T(4,128)} %bitcast.33), channel_id=1, replica_groups=mesh['row'=16,'col'=32] {'col'}, dimensions={0}, use_global_device_ids=true | all-gather | bytes 540672 | tf_op jit(solution)/shard_map/all_gather | solution.py:24
  47.2 0.1 broadcast_select_fusion
  47.3 0.2 reshape.18
  47.5 1.2 reshape.10
  48.8 0.0 all-reduce.4.cloned.1.call-update
  48.8 0.0 all-reduce.6.cloned.1.call-start
  49.6 0.0 copy-done.3
  49.6 128.2 %all-reduce.4.cloned.1.call-done = f32[4,2,128,128]{2,1,0,3:T(2,128)} async-done(((f32[4,2,128,128]{2,1,0,3:T(2,128)}), f32[4,2,128,128]{2,1,0,3:T(2,128)}) %all-reduce.4.cloned.1.call-update) | async-done | bytes 524304 | tf_op jit(solution)/shard_map/psum | solution.py:9
  177.8 1.9 dynamic-slice_reduce_fusion
  179.6 0.0 copy-done
  179.7 0.0 copy-start.2
  179.7 3.1 fusion.1
  182.8 0.0 all-reduce.6.cloned.1.call-update
  182.8 1.3 dynamic-slice
  184.7 151.8 %all-reduce.6.cloned.1.call-done = f32[1024,128]{0,1:T(8,128)} async-done(((f32[1024,128]{0,1:T(8,128)}), f32[1024,128]{0,1:T(8,128)}) %all-reduce.6.cloned.1.call-update) | async-done | bytes 524304
  336.5 0.8 dynamic-slice_bitcast_fusion
  337.3 36.0 %all-gather.1 = f32[32,4,1024]{2,1,0:T(4,128)S(1)} all-gather(f32[1,4,1024]{2,1,0:T(4,128)S(1)} %dynamic-slice_bitcast_fusion), channel_id=1, replica_groups=mesh['row'=16,'col'=32] {'col'}, dimensions={0}, use_global_device_ids=true | all-gather | bytes 540672 | tf_op jit(solution)/shard_map/all_gather | solution.py:43
  373.2 0.2 reshape.15
  373.4 0.5 fusion.8
  374.0 60.4 %psum.15 = f32[128,4]{1,0:T(8,128)S(1)} all-reduce(f32[128,4]{1,0:T(8,128)S(1)} %fusion.8), channel_id=1, replica_groups=mesh['row'=16,'col'=32] {'row'}, use_global_device_ids=true, to_apply=%region_2.3 | all-reduce | flops 512 | bytes 4096 | tf_op jit(solution)/shard_map/psum | solution.py:54
  434.4 1.0 fusion.5
  435.4 0.8 fusion.2
  (6 shorter events, 0.1 us)
Async XLA Ops:
  7.2 172.5 %copy-start = (f32[1024,512]{1,0:T(8,128)S(1)}, f32[1024,512]{1,0:T(8,128)}, u32[]{:S(2)}) copy-start(f32[1024,512]{1,0:T(8,128)} %param.5) | copy-start | bytes 6291460
  7.2 170.6 %all-reduce.4.cloned.1.call-start = ((), (), s32[]{:S(2)}) async-start(), calls=%async_computation | async-start | bytes 1048576 | tf_op jit(solution)/shard_map/psum | solution.py:9
  47.2 2.4 copy-start.3
  48.8 287.7 %all-reduce.6.cloned.1.call-start = ((), (), s32[]{:S(2)}) async-start(), calls=%async_computation.1 | async-start | bytes 1048576
  179.7 193.8 %copy-start.2 = (f32[1024,4]{0,1:T(4,128)S(1)}, f32[1024,4]{0,1:T(4,128)}, u32[]{:S(2)}) copy-start(f32[1024,4]{0,1:T(4,128)} %param.6) | copy-start | bytes 49156
  182.8 251.6 %copy-start.1 = (f32[128,128]{1,0:T(8,128)S(1)}, f32[128,128]{1,0:T(8,128)}, u32[]{:S(2)}) copy-start(f32[128,128]{1,0:T(8,128)} %param.8) | copy-start | bytes 196612
Sparse Core Ops, SparseCore 0:
  48.9 128.8 all-reduce.3
  182.9 153.5 all-reduce.5
where the time goes:
time: 445 us; the launch traced here: 443 us
  waiting for transfers between devices  280 us (63%)
  blocking collectives  136 us (31%)
  between operations  15.5 us (3%)
  local copies, waits for them, and re-layouts  5.58 us (1%)
  matrix products  5.52 us (1%)
    unnamed x3, waiting for transfers between devices  152 us
    psum x1, waiting for transfers between devices, broadcast(): return lax.psum(jnp.where(mine, value, jnp.zeros_like(value)), axis)  128 us
    psum x1, blocking collectives, body(): gram_total = lax.psum(gram_local, 'row')  60.4 us
    all_gather x1, blocking collectives, body(): panel_rows = lax.all_gather(panel, 'col', axis=1, tiled=True)  40 us
    all_gather x1, blocking collectives, body(): full_rows = lax.all_gather(thin_part, 'col', axis=1, tiled=True)  36 us
  transfers between devices with their start and end apart: 2, of which 2 were waited for; matrix products, arithmetic and copies ran while one was open for 0% of the time, Pallas kernels for 0%

commit v1 on v0

v1 whole, which is shorter than its diff:
```python
import jax
import jax.numpy as jnp
from jax import lax
from jax.sharding import PartitionSpec as P

HIGH = lax.Precision.HIGHEST


def dot(a, b, contract):
    return lax.dot_general(
        a, b, (contract, ((), ())), precision=HIGH, preferred_element_type=jnp.float32
    )


def exchange(value, axis):
    return lax.all_to_all(value, axis, split_axis=0, concat_axis=0)


def body(trail_adjoint, panel, panel_adjoint, inv_diag, panel_index):
    rows_here, thin_cols = panel.shape
    width = inv_diag.shape[0]
    ways_row = lax.axis_size("row")
    ways_col = lax.axis_size("col")
    ratio = ways_col // ways_row
    cols_here = trail_adjoint.shape[1]
    col_here = lax.axis_index("col")
    thin = panel.T
    everywhere = exchange(jnp.broadcast_to(thin[None], (ways_row, thin_cols, rows_here)), "row")
    parts = everywhere.reshape(ways_row, thin_cols, cols_here // width, ratio, width)
    targets = jnp.arange(ways_col, dtype=jnp.int32).reshape(ratio, ways_row)
    offset = jnp.mod(targets - panel_index[0] - 1, ways_col) // ways_row
    offset = offset[:, :, None, None, None]
    chosen = jnp.zeros((ratio, ways_row, thin_cols, cols_here // width, width), jnp.float32)
    for i in range(ratio):
        chosen = jnp.where(offset == i, parts[None, :, :, :, i], chosen)
    chosen = chosen.reshape(ways_col, thin_cols, cols_here)
    sent = jnp.concatenate(
        [chosen, jnp.broadcast_to(thin[None], (ways_col, thin_cols, rows_here))], axis=2
    )
    got = exchange(sent, "col").reshape(width, cols_here + rows_here)
    column_panel = got[:, :cols_here]
    panel_rows = got[:, cols_here:]
    scaled = dot(inv_diag, column_panel, ((0,), (0,)))
    product = dot(scaled, trail_adjoint, ((1,), (1,)))
    my_inverse = lax.dynamic_slice_in_dim(inv_diag, col_here * thin_cols, thin_cols, 0)
    local = dot(my_inverse, panel_adjoint.T, ((0,), (0,))) - 2.0 * product
    diag = -dot(panel_rows, local, ((1,), (1,)))
    both = jnp.concatenate([local, diag], axis=1).reshape(ways_col, thin_cols, rows_here + width)
    total = jnp.sum(exchange(both, "col"), axis=0)
    panel_grad = total[:, :rows_here].T
    mine = jnp.broadcast_to(total[None, :, rows_here:], (ways_row, thin_cols, width))
    diag_grad = jnp.sum(exchange(mine, "row"), axis=0).T
    return (panel_grad, diag_grad)


def solution(mesh):
    in_specs = (P("row", "col"), P("row", "col"), P("row", "col"), P(), P())
    out_specs = (P("row", "col"), P(None, "col"))
    return jax.shard_map(body, mesh=mesh, in_specs=in_specs, out_specs=out_specs, check_vma=False)
```

time: 445 us -> 104 us (0.23)
  waiting for transfers between devices: 280 us -> 39.5 us
  blocking collectives: 136 us -> 21.7 us
  starting transfers between devices: 0.08 us -> 28.4 us
  between operations: 15.5 us -> 1.51 us
    unnamed x3 -> x0, waiting for transfers between devices: 152 us -> none
    psum x1 -> x0, waiting for transfers between devices: 128 us -> none  [broadcast(): return lax.psum(jnp.where(mine, value, jnp.zeros_like(value)), axis)]
    all_gather x2 -> x0, blocking collectives: 75.9 us -> none  [the longest x1 40 us: body(): panel_rows = lax.all_gather(panel, 'col', axis=1, tiled=True)]
    psum x1 -> x0, blocking collectives: 60.4 us -> none  [body(): gram_total = lax.psum(gram_local, 'row')]
    all_to_all x0 -> x3, waiting for transfers between devices: none -> 39.5 us  [exchange(): return lax.all_to_all(value, axis, split_axis=0, concat_axis=0)]
    all_to_all x0 -> x3, starting transfers between devices: none -> 28.4 us  [exchange(): return lax.all_to_all(value, axis, split_axis=0, concat_axis=0)]
    all_to_all x0 -> x1, blocking collectives: none -> 21.7 us  [exchange(): return lax.all_to_all(value, axis, split_axis=0, concat_axis=0)]
  transfers between devices with their start and end apart: 2 -> 3, of which waited for: 2 -> 3; matrix products, arithmetic and copies ran while one was open for 0% -> 1% of each run, Pallas kernels for 0% -> 0%
where the time goes in v1:
time: 104 us; the launch traced here: 103 us
  waiting for transfers between devices  39.5 us (38%)
  starting transfers between devices  28.4 us (27%)
  blocking collectives  21.7 us (21%)
  local copies, waits for them, and re-layouts  5.31 us (5%)
  matrix products  5.11 us (5%)
  other arithmetic  2.01 us (2%)
  between operations  1.51 us (1%)
    all_to_all x3, waiting for transfers between devices, exchange(): return lax.all_to_all(value, axis, split_axis=0, concat_axis=0)  39.5 us
    all_to_all x3, starting transfers between devices, exchange(): return lax.all_to_all(value, axis, split_axis=0, concat_axis=0)  28.4 us
    all_to_all x1, blocking collectives, exchange(): return lax.all_to_all(value, axis, split_axis=0, concat_axis=0)  21.7 us
    dot_general x4, matrix products, dot(): lax.dot_general(a, b, (contract, ((), ())), precision=HIGH, preferred_ele...  5.11 us
  transfers between devices with their start and end apart: 3, of which 3 were waited for; matrix products, arithmetic and copies ran while one was open for 1% of the time, Pallas kernels for 0%

profile of v1, /device:TPU:1, one launch (start us, length us, event | category | flops | bytes accessed | tf_op | source)
XLA Modules:
  0.0 103.5 jit_solution(6884384928322448492)
XLA Ops:
  0.6 1.6 %broadcast_in_dim.57 = f32[16,4,1024]{2,1,0:T(4,128)} broadcast(f32[4,1024]{1,0:T(4,128)} %bitcast.15), dimensions={1,2} | broadcast | bytes 278528 | tf_op jit(solution)/shard_map/broadcast_in_dim | solution.py:28
  2.3 11.8 %all-to-all-start = ((f32[16,4,1024]{2,1,0:T(4,128)}), f32[16,4,1024]{2,1,0:T(4,128)S(1)}, u32[]{:S(2)}, u32[]{:S(2)}) async-start(f32[16,4,1024]{2,1,0:T(4,128)} %broadcast_in_dim.57), calls=%async_computation | async-start | bytes 524288 | tf_op jit(solution)/shard_map/all_to_all | solution.py:16
  14.9 10.9 %all-to-all-done = f32[16,4,1024]{2,1,0:T(4,128)S(1)} async-done(((f32[16,4,1024]{2,1,0:T(4,128)}), f32[16,4,1024]{2,1,0:T(4,128)S(1)}, u32[]{:S(2)}, u32[]{:S(2)}) %all-to-all-start) | async-done | bytes 262176 | tf_op jit(solution)/shard_map/all_to_all | solution.py:16
  25.8 0.3 reshape.88
  26.1 0.2 fusion.6
  26.4 0.2 broadcast_in_dim.60
  26.7 0.2 broadcast_in_dim.64
  26.8 0.2 select_select_fusion
  27.0 0.1 broadcast_in_dim.66
  27.1 1.1 %pad_maximum_fusion = f32[32,4,1536]{2,1,0:T(4,128)} fusion(f32[32,4,1024]{2,1,0:T(4,128)S(1)} %broadcast_in_dim.66, f32[32,4,512]{2,1,0:T(4,128)S(1)} %select_select_fusion), kind=kLoop, calls=%fused_computation.3 | loop fusion | flops 196608 | bytes 1572864 | tf_op jit(solution)/shard_map/concatenate | solution.py:37
  28.2 9.7 %all-to-all-start.1 = ((f32[32,4,1536]{2,1,0:T(4,128)}), f32[32,4,1536]{2,1,0:T(4,128)S(1)}, u32[]{:S(2)}, u32[]{:S(2)}) async-start(f32[32,4,1536]{2,1,0:T(4,128)} %pad_maximum_fusion), calls=%async_computation.1 | async-start | bytes 1572864 | tf_op jit(solution)/shard_map/all_to_all | solution.py:16
  37.9 21.7 %all-to-all-done.1 = f32[32,4,1536]{2,1,0:T(4,128)S(1)} async-done(((f32[32,4,1536]{2,1,0:T(4,128)}), f32[32,4,1536]{2,1,0:T(4,128)S(1)}, u32[]{:S(2)}, u32[]{:S(2)}) %all-to-all-start.1) | async-done | bytes 786464 | tf_op jit(solution)/shard_map/all_to_all | solution.py:16
  59.5 1.2 %reshape.86 = f32[128,1536]{1,0:T(8,128)} reshape(f32[32,4,1536]{2,1,0:T(4,128)S(1)} %all-to-all-done.1) | data formatting | bytes 1572864 | tf_op jit(solution)/shard_map/reshape | solution.py:40
  60.7 1.5 %fusion.1 = f32[512,128]{1,0:T(8,128)S(1)} fusion(f32[128,128]{1,0:T(8,128)S(1)} %copy-done.2, f32[128,1536]{1,0:T(8,128)} %reshape.86), kind=kOutput, calls=%fused_computation.6 | convolution fusion | flops 100663296 | bytes 589824 | tf_op jit(solution)/shard_map/dot_general | solution.py:10
  62.3 2.3 %convolution_multiply_fusion = f32[128,1024]{1,0:T(8,128)S(1)} fusion(f32[512,128]{1,0:T(8,128)S(1)} %fusion.1, f32[1024,512]{1,0:T(8,128)S(1)} %copy-done), kind=kOutput, calls=%fused_computation.1 | convolution fusion | flops 805437440 | bytes 2883584 | tf_op jit(solution)/shard_map/dot_general | solution.py:10
  64.6 0.7 convolution_subtract_fusion
  65.3 0.6 convolution_negate_fusion
  65.9 0.2 reshape.87
  66.1 21.7 %all_to_all.20 = f32[32,4,1152]{2,1,0:T(4,128)S(1)} all-to-all(f32[32,4,1152]{2,1,0:T(4,128)S(1)} %reshape.87), channel_id=1, replica_groups=mesh['row'=16,'col'=32] {'col'}, dimensions={0} | all-to-all | bytes 1179648 | tf_op jit(solution)/shard_map/all_to_all | solution.py:16
  87.9 0.6 broadcast_in_dim.67
  88.5 6.9 %all-to-all-start.3 = ((f32[16,4,128]{2,1,0:T(4,128)}), f32[16,4,128]{2,1,0:T(4,128)S(1)}, u32[]{:S(2)}, u32[]{:S(2)}) async-start(f32[16,4,128]{2,1,0:T(4,128)} %broadcast_in_dim.67), calls=%async_computation.3 | async-start | bytes 65536 | tf_op jit(solution)/shard_map/all_to_all | solution.py:16
  95.4 0.6 slice_bitcast_fusion
  96.0 6.9 %all-to-all-done.3 = f32[16,4,128]{2,1,0:T(4,128)S(1)} async-done(((f32[16,4,128]{2,1,0:T(4,128)}), f32[16,4,128]{2,1,0:T(4,128)S(1)}, u32[]{:S(2)}, u32[]{:S(2)}) %all-to-all-start.3) | async-done | bytes 32800 | tf_op jit(solution)/shard_map/all_to_all | solution.py:16
  102.9 0.6 reduce_sum.19
  (23 shorter events, 0.5 us)
Async XLA Ops:
  0.6 61.6 %copy-start = (f32[1024,512]{1,0:T(8,128)S(1)}, f32[1024,512]{1,0:T(8,128)}, u32[]{:S(2)}) copy-start(f32[1024,512]{1,0:T(8,128)} %param.5) | copy-start | bytes 6291460
  2.3 23.5 %all-to-all-start = ((f32[16,4,1024]{2,1,0:T(4,128)}), f32[16,4,1024]{2,1,0:T(4,128)S(1)}, u32[]{:S(2)}, u32[]{:S(2)}) async-start(f32[16,4,1024]{2,1,0:T(4,128)} %broadcast_in_dim.57), calls=%async_computation | async-start | bytes 524288 | tf_op jit(solution)/shard_map/all_to_all | solution.py:16
  26.1 0.9 copy-start.3
  27.1 33.6 %copy-start.2 = (f32[128,128]{1,0:T(8,128)S(1)}, f32[128,128]{1,0:T(8,128)}, u32[]{:S(2)}) copy-start(f32[128,128]{1,0:T(8,128)} %param.8) | copy-start | bytes 196612
  28.2 31.3 %all-to-all-start.1 = ((f32[32,4,1536]{2,1,0:T(4,128)}), f32[32,4,1536]{2,1,0:T(4,128)S(1)}, u32[]{:S(2)}, u32[]{:S(2)}) async-start(f32[32,4,1536]{2,1,0:T(4,128)} %pad_maximum_fusion), calls=%async_computation.1 | async-start | bytes 1572864 | tf_op jit(solution)/shard_map/all_to_all | solution.py:16
  60.7 3.9 %copy-start.4 = (f32[1024,4]{0,1:T(4,128)S(1)}, f32[1024,4]{0,1:T(4,128)}, u32[]{:S(2)}) copy-start(f32[1024,4]{0,1:T(4,128)} %param.7) | copy-start | bytes 49156
  62.3 3.0 %copy-start.1 = (f32[128,1536]{1,0:T(8,128)S(1)}, f32[128,1536]{1,0:T(8,128)}, u32[]{:S(2)}) copy-start(f32[128,1536]{1,0:T(8,128)} %reshape.86) | copy-start | bytes 2359300
  88.5 14.4 %all-to-all-start.3 = ((f32[16,4,128]{2,1,0:T(4,128)}), f32[16,4,128]{2,1,0:T(4,128)S(1)}, u32[]{:S(2)}, u32[]{:S(2)}) async-start(f32[16,4,128]{2,1,0:T(4,128)} %broadcast_in_dim.67), calls=%async_computation.3 | async-start | bytes 65536 | tf_op jit(solution)/shard_map/all_to_all | solution.py:16

commit v2 on v1

v2 whole, which is shorter than its diff:
```python
import jax
import jax.numpy as jnp
from jax import lax
from jax.experimental import pallas as pl
from jax.experimental.pallas import tpu as pltpu
from jax.sharding import PartitionSpec as P

X_WAYS = 4
F32 = jnp.float32


def exchange(value, axis, groups=None):
    return lax.all_to_all(value, axis, split_axis=0, concat_axis=0, axis_index_groups=groups)


def halves(value):
    high = value.astype(jnp.bfloat16)
    low = (value - high.astype(F32)).astype(jnp.bfloat16)
    return high, low


def dot(a, b, contract):
    a_high, a_low = halves(a)
    b_high, b_low = halves(b)

    def one(p, q):
        return lax.dot_general(p, q, (contract, ((), ())), preferred_element_type=F32)

    return one(a_high, b_high) + (one(a_high, b_low) + one(a_low, b_high))


def call(kernel, shapes, *args, scalars=0):
    vmem = pl.BlockSpec(memory_space=pltpu.VMEM)
    smem = pl.BlockSpec(memory_space=pltpu.SMEM)
    single = not isinstance(shapes, (list, tuple))
    outs = [shapes] if single else list(shapes)
    got = pl.pallas_call(
        kernel,
        out_shape=[jax.ShapeDtypeStruct(s, F32) for s in map(tuple, (o.shape for o in outs))],
        in_specs=[smem] * scalars + [vmem] * (len(args) - scalars),
        out_specs=[vmem] * len(outs),
        compiler_params=pltpu.CompilerParams(vmem_limit_bytes=48 << 20),
    )(*args)
    return got[0] if single else got


def like(*shape):
    return jax.ShapeDtypeStruct(shape, F32)


def spread(index_ref, thin_ref, out_ref, *, width, ratio):
    row = lax.axis_index("row")
    ways_row = out_ref.shape[0]
    ways_col = ratio * ways_row
    half = thin_ref.shape[1] // ratio
    for p in range(ratio):
        column = row + p * ways_row
        offset = lax.rem(column + 2048 * ways_col - index_ref[0] - 1, ways_col) // ways_row
        for j in range(half // width):
            at = ratio * j * width
            piece = thin_ref[:, at : at + width]
            for i in range(1, ratio):
                piece = jnp.where(offset == i, thin_ref[:, at + i * width : at + (i + 1) * width], piece)
            for r in range(ways_row):
                out_ref[r, :, p * half + j * width : p * half + (j + 1) * width] = piece


def route(every_ref, thin_ref, out_ref):
    ways_row = every_ref.shape[0]
    ways_col = out_ref.shape[0]
    quarter = thin_ref.shape[1] // X_WAYS
    cols = out_ref.shape[2] - quarter
    for c in range(ways_col):
        p = c // ways_row
        x = c // (ways_col // X_WAYS)
        out_ref[c, :, :cols] = every_ref[c % ways_row, :, p * cols : (p + 1) * cols]
        out_ref[c, :, cols:] = thin_ref[:, x * quarter : (x + 1) * quarter]


def multiply(got_ref, trail_ref, adjoint_ref, inv_ref, out_ref, panel_ref, work_ref):
    ways_col, thin_cols, _ = got_ref.shape
    rows_here, cols = trail_ref.shape
    for c in range(ways_col):
        work_ref[c * thin_cols : (c + 1) * thin_cols, :] = got_ref[c]
    inv = inv_ref[...]
    scaled = dot(inv.T * -2.0, work_ref[:, :cols], ((1,), (0,)))
    panel_ref[...] = work_ref[:, cols:]
    col = lax.axis_index("col")
    mine = inv_ref[pl.ds(col * thin_cols, thin_cols), :].T
    quarter = rows_here // X_WAYS
    for x in range(X_WAYS):
        at = slice(x * quarter, (x + 1) * quarter)
        local = dot(scaled, trail_ref[at, :], ((1,), (1,)))
        for i in range(thin_cols):
            local = local + mine[:, i : i + 1] * adjoint_ref[i : i + 1, at]
        out_ref[x] = local


def gram(parts_ref, panel_ref, out_ref):
    ways_col, thin_cols, _ = out_ref.shape
    total = parts_ref[0]
    for x in range(1, X_WAYS):
        total = total + parts_ref[x]
    quarter = total.shape[1]
    diag = dot(-panel_ref[...], total, ((1,), (1,)))
    for c in range(ways_col):
        at = slice(c * thin_cols, (c + 1) * thin_cols)
        out_ref[c, :, :quarter] = total[at, :]
        out_ref[c, :, quarter:] = diag[at, :]


def finish(parts_ref, grad_ref, out_ref):
    ways_col = parts_ref.shape[0]
    y_ways = ways_col // X_WAYS
    quarter = grad_ref.shape[1] // X_WAYS
    diag = None
    for x in range(X_WAYS):
        total = parts_ref[x * y_ways]
        for y in range(1, y_ways):
            total = total + parts_ref[x * y_ways + y]
        grad_ref[:, x * quarter : (x + 1) * quarter] = total[:, :quarter]
        diag = total[:, quarter:] if diag is None else diag + total[:, quarter:]
    for r in range(out_ref.shape[0]):
        out_ref[r] = diag


def last(parts_ref, out_ref):
    total = parts_ref[0]
    for r in range(1, parts_ref.shape[0]):
        total = total + parts_ref[r]
    out_ref[...] = total


def body(trail_adjoint, panel, panel_adjoint, inv_diag, panel_index):
    rows_here, thin_cols = panel.shape
    width = inv_diag.shape[0]
    ways_row = lax.axis_size("row")
    ways_col = lax.axis_size("col")
    cols = trail_adjoint.shape[1]
    quarter = rows_here // X_WAYS
    y_ways = ways_col // X_WAYS
    groups = [[x * y_ways + y for x in range(X_WAYS)] for y in range(y_ways)]
    thin = panel.T

    def spreading(*refs):
        spread(*refs, width=width, ratio=ways_col // ways_row)

    copies = call(spreading, like(ways_row, thin_cols, rows_here), panel_index, thin, scalars=1)
    sent = call(route, like(ways_col, thin_cols, cols + quarter), exchange(copies, "row"), thin)
    got = exchange(sent, "col")
    vmem = pl.BlockSpec(memory_space=pltpu.VMEM)
    parts, panel_rows = pl.pallas_call(
        multiply,
        out_shape=[like(X_WAYS, width, quarter), like(width, quarter)],
        in_specs=[vmem] * 4,
        out_specs=[vmem] * 2,
        scratch_shapes=[pltpu.VMEM((width, cols + quarter), F32)],
        compiler_params=pltpu.CompilerParams(vmem_limit_bytes=48 << 20),
    )(got, trail_adjoint, panel_adjoint.T, inv_diag)
    both = call(gram, like(ways_col, thin_cols, quarter + width), exchange(parts, "col", groups), panel_rows)
    grad, mine = call(
        finish, [like(thin_cols, rows_here), like(ways_row, thin_cols, width)], exchange(both, "col")
    )
    diag = call(last, like(thin_cols, width), exchange(mine, "row"))
    return (grad.T, diag.T)


def solution(mesh):
    in_specs = (P("row", "col"), P("row", "col"), P("row", "col"), P(), P())
    out_specs = (P("row", "col"), P(None, "col"))
    return jax.shard_map(body, mesh=mesh, in_specs=in_specs, out_specs=out_specs, check_vma=False)
```

time: 104 us -> 91.3 us (0.88)
  blocking collectives: 21.7 us -> 85.7 us
  waiting for transfers between devices: 39.5 us -> 0 us
  starting transfers between devices: 28.4 us -> 0 us
  matrix products: 5.11 us -> 0 us
  local copies, waits for them, and re-layouts: 5.31 us -> 0.72 us
  Pallas kernels: 0 us -> 3 us
  other arithmetic: 2.01 us -> 0 us
    all_to_all x1 -> x5, blocking collectives: 21.7 us -> 85.7 us  [exchange(): lax.all_to_all(value, axis, split_axis=0, concat_axis=0, axis_index_group...]
    all_to_all x3 -> x0, waiting for transfers between devices: 39.5 us -> none  [exchange(): return lax.all_to_all(value, axis, split_axis=0, concat_axis=0)]
    all_to_all x3 -> x0, starting transfers between devices: 28.4 us -> none  [exchange(): return lax.all_to_all(value, axis, split_axis=0, concat_axis=0)]
    dot_general x4 -> x0, matrix products: 5.11 us -> none  [dot(): lax.dot_general(a, b, (contract, ((), ())), precision=HIGH, preferred_ele...]
    pallas_call x0 -> x6, Pallas kernels: none -> 3 us  [the longest x5 1.5 us: call(): pl.pallas_call(kernel, out_shape=[jax.ShapeDtypeStruct(s, F32) for s in m...]
    broadcast_in_dim x9 -> x0, local copies, waits for them, and re-layouts: 2.75 us -> none  [the longest x1 1.62 us: body(): jnp.broadcast_to(thin[None], (ways_row, thin_cols, rows_here))]
    reshape x3 -> x0, local copies, waits for them, and re-layouts: 1.58 us -> none  [the longest x1 1.15 us: body(): got = exchange(sent, 'col').reshape(width, cols_here + rows_here)]
    concatenate x2 -> x0, other arithmetic: 1.12 us -> none  [the longest x1 1.07 us: body(): jnp.concatenate([chosen, jnp.broadcast_to(thin[None], (ways_col, thin_col...]
  transfers between devices with their start and end apart: 3 -> 0, of which waited for: 3 -> 0; matrix products, arithmetic and copies ran while one was open for 1% -> 0% of each run, Pallas kernels for 0% -> 0%
where the time goes in v2:
time: 91.3 us; the launch traced here: 90.9 us
  blocking collectives  85.7 us (94%)
  Pallas kernels  3 us (3%)
  between operations  1.48 us (2%)
    all_to_all x5, blocking collectives, exchange(): lax.all_to_all(value, axis, split_axis=0, concat_axis=0, axis_index_group...  85.7 us

profile of v2, /device:TPU:1, one launch (start us, length us, event | category | flops | bytes accessed | tf_op | source)
XLA Modules:
  0.0 90.9 jit_solution(2008938384202332176)
XLA Ops:
  0.6 0.0 copy-start.1
  0.6 0.0 copy-start
  1.4 0.0 copy-start.2
  1.5 0.7 copy-done.2
  2.2 0.0 copy-start.3
  2.2 23.3 %all_to_all.25.every_ref = f32[16,4,1024]{2,1,0:T(4,128)S(1)} all-to-all(f32[16,4,1024]{2,1,0:T(4,128)S(1)} %shard_map.68), channel_id=1, replica_groups=mesh['row'=16,'col'=32] {'row'}, dimensions={0} | all-to-all | bytes 524288 | tf_op jit(solution)/shard_map/all_to_all | solution.py:13
  25.6 22.8 %all_to_all.26.got_ref = f32[32,4,768]{2,1,0:T(4,128)S(1)} all-to-all(f32[32,4,768]{2,1,0:T(4,128)S(1)} %shard_map.69), channel_id=1, replica_groups=mesh['row'=16,'col'=32] {'col'}, dimensions={0} | all-to-all | bytes 786432 | tf_op jit(solution)/shard_map/all_to_all | solution.py:13
  48.4 0.0 copy-done.1
  48.4 0.0 copy-done
  48.4 0.0 copy-done.3
  48.4 1.5 %shard_map.70 = (f32[4,128,256]{2,1,0:T(8,128)S(1)}, f32[128,256]{1,0:T(8,128)S(1)}) custom-call(f32[32,4,768]{2,1,0:T(4,128)S(1)} %all_to_all.26.got_ref, f32[1024,512]{1,0:T(8,128)S(1)} %copy-done, f32[4,1024]{1,0:T(4,128)S(1)} %bitcast.6, f32[128,128]{1,0:T(8,128)S(1)} %copy-done.1), custom_call_target="tpu_custom_call" | custom-call | tf_op jit(solution)/shard_map/pallas_call | solution.py:152
  49.9 10.6 %all_to_all.27.parts_ref = f32[4,128,256]{2,1,0:T(8,128)S(1)} all-to-all(f32[4,128,256]{2,1,0:T(8,128)S(1)} %get-tuple-element.6), channel_id=1, replica_groups={{0,8,16,24},{1,9,17,25},{2,10,18,26},{3,11,19,27},{4,12,20,28},{5,13,21..., dimensions={0} | all-to-all | bytes 1048576 | tf_op jit(solution)/shard_map/all_to_all | solution.py:13
  60.5 0.2 shard_map.71
  60.7 15.4 %all_to_all.28.parts_ref = f32[32,4,384]{2,1,0:T(4,128)S(1)} all-to-all(f32[32,4,384]{2,1,0:T(4,128)S(1)} %shard_map.71), channel_id=1, replica_groups=mesh['row'=16,'col'=32] {'col'}, dimensions={0} | all-to-all | bytes 393216 | tf_op jit(solution)/shard_map/all_to_all | solution.py:13
  76.1 0.6 shard_map.72
  76.7 13.6 %all_to_all.29.parts_ref = f32[16,4,128]{2,1,0:T(4,128)S(1)} all-to-all(f32[16,4,128]{2,1,0:T(4,128)S(1)} %get-tuple-element.9), channel_id=1, replica_groups=mesh['row'=16,'col'=32] {'row'}, dimensions={0} | all-to-all | bytes 65536 | tf_op jit(solution)/shard_map/all_to_all | solution.py:13
  90.3 0.6 shard_map.73
  (2 shorter events, 0.1 us)
Async XLA Ops:
  0.6 47.7 %copy-start.1 = (f32[128,128]{1,0:T(8,128)S(1)}, f32[128,128]{1,0:T(8,128)}, u32[]{:S(2)}) copy-start(f32[128,128]{1,0:T(8,128)} %inv_ref.1) | copy-start | bytes 196612
  0.6 47.7 %copy-start = (f32[1024,512]{1,0:T(8,128)S(1)}, f32[1024,512]{1,0:T(8,128)}, u32[]{:S(2)}) copy-start(f32[1024,512]{1,0:T(8,128)} %trail_ref.1) | copy-start | bytes 6291460
  1.4 0.7 copy-start.2
  2.2 46.2 %copy-start.3 = (f32[1024,4]{0,1:T(4,128)S(1)}, f32[1024,4]{0,1:T(4,128)}, u32[]{:S(2)}) copy-start(f32[1024,4]{0,1:T(4,128)} %param.7) | copy-start | bytes 49156

commit v3 on v2

--- a/solution.py
+++ b/solution.py
@@ -6,6 +6,7 @@
 from jax.sharding import PartitionSpec as P
 
 X_WAYS = 4
+CORES = 2
 F32 = jnp.float32
 
 
@@ -52,39 +53,44 @@
     row = lax.axis_index("row")
     ways_row = out_ref.shape[0]
     ways_col = ratio * ways_row
-    half = thin_ref.shape[1] // ratio
+    share = out_ref.shape[2] // ratio
+    blocks = share // width
     for p in range(ratio):
         column = row + p * ways_row
         offset = lax.rem(column + 2048 * ways_col - index_ref[0] - 1, ways_col) // ways_row
-        for j in range(half // width):
+        for j in range(CORES * blocks):
             at = ratio * j * width
             piece = thin_ref[:, at : at + width]
             for i in range(1, ratio):
                 piece = jnp.where(offset == i, thin_ref[:, at + i * width : at + (i + 1) * width], piece)
-            for r in range(ways_row):
-                out_ref[r, :, p * half + j * width : p * half + (j + 1) * width] = piece
+            to = p * share + j % blocks * width
+            for r in range(j // blocks, ways_row, CORES):
+                out_ref[r, :, to : to + width] = piece
 
 
 def route(every_ref, thin_ref, out_ref):
     ways_row = every_ref.shape[0]
     ways_col = out_ref.shape[0]
     quarter = thin_ref.shape[1] // X_WAYS
-    cols = out_ref.shape[2] - quarter
+    share = out_ref.shape[2] - quarter
     for c in range(ways_col):
         p = c // ways_row
         x = c // (ways_col // X_WAYS)
-        out_ref[c, :, :cols] = every_ref[c % ways_row, :, p * cols : (p + 1) * cols]
-        out_ref[c, :, cols:] = thin_ref[:, x * quarter : (x + 1) * quarter]
+        out_ref[c, :, :share] = every_ref[c % ways_row, :, p * share : (p + 1) * share]
+        out_ref[c, :, share:] = thin_ref[:, x * quarter : (x + 1) * quarter]
 
 
-def multiply(got_ref, trail_ref, adjoint_ref, inv_ref, out_ref, panel_ref, work_ref):
+def multiply(pair_ref, got_ref, trail_ref, adjoint_ref, inv_ref, out_ref, panel_ref, work_ref):
     ways_col, thin_cols, _ = got_ref.shape
     rows_here, cols = trail_ref.shape
+    share = cols // CORES
     for c in range(ways_col):
-        work_ref[c * thin_cols : (c + 1) * thin_cols, :] = got_ref[c]
+        at = slice(c * thin_cols, (c + 1) * thin_cols)
+        for core in range(CORES):
+            work_ref[at, core * share : (core + 1) * share] = pair_ref[core, c, :, :share]
+        panel_ref[at, :] = got_ref[c, :, share:]
     inv = inv_ref[...]
-    scaled = dot(inv.T * -2.0, work_ref[:, :cols], ((1,), (0,)))
-    panel_ref[...] = work_ref[:, cols:]
+    scaled = dot(inv.T * -2.0, work_ref[...], ((1,), (0,)))
     col = lax.axis_index("col")
     mine = inv_ref[pl.ds(col * thin_cols, thin_cols), :].T
     quarter = rows_here // X_WAYS
@@ -145,18 +151,21 @@
     def spreading(*refs):
         spread(*refs, width=width, ratio=ways_col // ways_row)
 
-    copies = call(spreading, like(ways_row, thin_cols, rows_here), panel_index, thin, scalars=1)
-    sent = call(route, like(ways_col, thin_cols, cols + quarter), exchange(copies, "row"), thin)
+    share = cols // CORES
+    copies = call(spreading, like(ways_row, thin_cols, rows_here // CORES), panel_index, thin, scalars=1)
+    sent = call(route, like(ways_col, thin_cols, share + quarter), exchange(copies, "row"), thin)
     got = exchange(sent, "col")
+    chips = [list(range(r, r + CORES)) for r in range(0, ways_row, CORES)]
+    pair = lax.all_gather(got, "row", axis=0, axis_index_groups=chips)
     vmem = pl.BlockSpec(memory_space=pltpu.VMEM)
     parts, panel_rows = pl.pallas_call(
         multiply,
         out_shape=[like(X_WAYS, width, quarter), like(width, quarter)],
-        in_specs=[vmem] * 4,
+        in_specs=[vmem] * 5,
         out_specs=[vmem] * 2,
-        scratch_shapes=[pltpu.VMEM((width, cols + quarter), F32)],
+        scratch_shapes=[pltpu.VMEM((width, cols), F32)],
         compiler_params=pltpu.CompilerParams(vmem_limit_bytes=48 << 20),
-    )(got, trail_adjoint, panel_adjoint.T, inv_diag)
+    )(pair, got, trail_adjoint, panel_adjoint.T, inv_diag)
     both = call(gram, like(ways_col, thin_cols, quarter + width), exchange(parts, "col", groups), panel_rows)
     grad, mine = call(
         finish, [like(thin_cols, rows_here), like(ways_row, thin_cols, width)], exchange(both, "col")

time: 91.3 us -> 89.5 us (0.980)
  blocking collectives: 85.7 us -> 83.1 us
    all_to_all x5, blocking collectives: 85.7 us -> 79.5 us  [exchange(): lax.all_to_all(value, axis, split_axis=0, concat_axis=0, axis_index_group...]
    all_gather x0 -> x1, blocking collectives: none -> 3.52 us  [body(): pair = lax.all_gather(got, 'row', axis=0, axis_index_groups=chips)]
where the time goes in v3:
time: 89.5 us; the launch traced here: 89.1 us
  blocking collectives  83.1 us (93%)
  Pallas kernels  2.97 us (3%)
  local copies, waits for them, and re-layouts  1.56 us (2%)
  between operations  1.47 us (2%)
    all_to_all x5, blocking collectives, exchange(): lax.all_to_all(value, axis, split_axis=0, concat_axis=0, axis_index_group...  79.5 us
    all_gather x1, blocking collectives, body(): pair = lax.all_gather(got, 'row', axis=0, axis_index_groups=chips)  3.52 us

profile of v3, /device:TPU:1, one launch (start us, length us, event | category | flops | bytes accessed | tf_op | source)
XLA Modules:
  0.0 89.1 jit_solution(5650339485139290066)
XLA Ops:
  0.6 0.0 copy-start
  1.4 0.0 copy-start.2
  1.4 0.7 copy-done.2
  2.2 0.0 copy-start.3
  2.2 20.8 %all_to_all.25.every_ref = f32[16,4,512]{2,1,0:T(4,128)S(1)} all-to-all(f32[16,4,512]{2,1,0:T(4,128)S(1)} %shard_map.68), channel_id=1, replica_groups=mesh['row'=16,'col'=32] {'row'}, dimensions={0} | all-to-all | bytes 262144 | tf_op jit(solution)/shard_map/all_to_all | solution.py:14
  23.0 20.2 %all_to_all.26.got_ref = f32[32,4,512]{2,1,0:T(4,128)S(1)} all-to-all(f32[32,4,512]{2,1,0:T(4,128)S(1)} %shard_map.69), channel_id=1, replica_groups=mesh['row'=16,'col'=32] {'col'}, dimensions={0} | all-to-all | bytes 524288 | tf_op jit(solution)/shard_map/all_to_all | solution.py:14
  43.2 3.5 %all-gather = f32[64,4,512]{2,1,0:T(4,128)S(1)} all-gather(f32[32,4,512]{2,1,0:T(4,128)S(1)} %all_to_all.26.got_ref), channel_id=2, replica_groups={{0,32},{64,96},{128,160},{192,224},{256,288},{320,352},{384,416},{448,4..., dimensions={0}, use_global_device_ids=true | all-gather | bytes 786432 | tf_op jit(solution)/shard_map/all_gather | solution.py:159
  46.7 0.0 copy-done
  46.7 0.0 copy-done.3
  46.7 0.0 copy-start.1
  46.7 0.8 copy-done.1
  47.5 1.5 %shard_map.70 = (f32[4,128,256]{2,1,0:T(8,128)S(1)}, f32[128,256]{1,0:T(8,128)S(1)}) custom-call(f32[2,32,4,512]{3,2,1,0:T(4,128)S(1)} %bitcast.5, f32[32,4,512]{2,1,0:T(4,128)S(1)} %all_to_all.26.got_ref, f32[1024,512]{1,0:T(8,128)S(1)} %copy-done, f32[4,1024]{1,0:T(4,128)S(1)} %bitcast.8, f32[128,128]{1,0:T(8,128)S(1)} %copy-done.1), custom_call_target="tpu_custom_call" | custom-call | tf_op jit(solution)/shard_map/pallas_call | solution.py:161
  49.0 11.7 %all_to_all.27.parts_ref = f32[4,128,256]{2,1,0:T(8,128)S(1)} all-to-all(f32[4,128,256]{2,1,0:T(8,128)S(1)} %get-tuple-element.6), channel_id=1, replica_groups={{0,8,16,24},{1,9,17,25},{2,10,18,26},{3,11,19,27},{4,12,20,28},{5,13,21..., dimensions={0} | all-to-all | bytes 1048576 | tf_op jit(solution)/shard_map/all_to_all | solution.py:14
  60.7 0.2 shard_map.71
  61.0 14.1 %all_to_all.28.parts_ref = f32[32,4,384]{2,1,0:T(4,128)S(1)} all-to-all(f32[32,4,384]{2,1,0:T(4,128)S(1)} %shard_map.71), channel_id=1, replica_groups=mesh['row'=16,'col'=32] {'col'}, dimensions={0} | all-to-all | bytes 393216 | tf_op jit(solution)/shard_map/all_to_all | solution.py:14
  75.0 0.6 shard_map.72
  75.7 12.8 %all_to_all.29.parts_ref = f32[16,4,128]{2,1,0:T(4,128)S(1)} all-to-all(f32[16,4,128]{2,1,0:T(4,128)S(1)} %get-tuple-element.9), channel_id=1, replica_groups=mesh['row'=16,'col'=32] {'row'}, dimensions={0} | all-to-all | bytes 65536 | tf_op jit(solution)/shard_map/all_to_all | solution.py:14
  88.5 0.6 shard_map.73
  (2 shorter events, 0.0 us)
Async XLA Ops:
  0.6 46.1 %copy-start = (f32[1024,512]{1,0:T(8,128)S(1)}, f32[1024,512]{1,0:T(8,128)}, u32[]{:S(2)}) copy-start(f32[1024,512]{1,0:T(8,128)} %trail_ref.1) | copy-start | bytes 6291460
  1.4 0.7 copy-start.2
  2.2 44.5 %copy-start.3 = (f32[1024,4]{0,1:T(4,128)S(1)}, f32[1024,4]{0,1:T(4,128)}, u32[]{:S(2)}) copy-start(f32[1024,4]{0,1:T(4,128)} %param.7) | copy-start | bytes 49156
  46.7 0.8 copy-start.1

commit v4 on v3

--- a/solution.py
+++ b/solution.py
@@ -80,7 +80,7 @@
         out_ref[c, :, share:] = thin_ref[:, x * quarter : (x + 1) * quarter]
 
 
-def multiply(pair_ref, got_ref, trail_ref, adjoint_ref, inv_ref, out_ref, panel_ref, work_ref):
+def multiply(pair_ref, got_ref, trail_ref, adjoint_ref, out_ref, panel_ref, work_ref):
     ways_col, thin_cols, _ = got_ref.shape
     rows_here, cols = trail_ref.shape
     share = cols // CORES
@@ -89,24 +89,26 @@
         for core in range(CORES):
             work_ref[at, core * share : (core + 1) * share] = pair_ref[core, c, :, :share]
         panel_ref[at, :] = got_ref[c, :, share:]
-    inv = inv_ref[...]
-    scaled = dot(inv.T * -2.0, work_ref[...], ((1,), (0,)))
+    scaled = work_ref[...] * -2.0
+    per_eight = 8 // thin_cols
     col = lax.axis_index("col")
-    mine = inv_ref[pl.ds(col * thin_cols, thin_cols), :].T
+    eight = pl.ds(pl.multiple_of(col // per_eight * 8, 8), 8)
+    owner = lax.broadcasted_iota(jnp.int32, (8, rows_here // X_WAYS), 0) // thin_cols
     quarter = rows_here // X_WAYS
     for x in range(X_WAYS):
         at = slice(x * quarter, (x + 1) * quarter)
-        local = dot(scaled, trail_ref[at, :], ((1,), (1,)))
-        for i in range(thin_cols):
-            local = local + mine[:, i : i + 1] * adjoint_ref[i : i + 1, at]
-        out_ref[x] = local
+        out_ref[x] = dot(scaled, trail_ref[at, :], ((1,), (1,)))
+        added = jnp.concatenate([adjoint_ref[:, at]] * per_eight, axis=0)
+        added = jnp.where(owner == lax.rem(col, per_eight), added, jnp.zeros_like(added))
+        out_ref[x, eight, :] = out_ref[x, eight, :] + added
 
 
-def gram(parts_ref, panel_ref, out_ref):
+def gram(parts_ref, panel_ref, inv_ref, out_ref):
     ways_col, thin_cols, _ = out_ref.shape
     total = parts_ref[0]
     for x in range(1, X_WAYS):
         total = total + parts_ref[x]
+    total = dot(inv_ref[...].T, total, ((1,), (0,)))
     quarter = total.shape[1]
     diag = dot(-panel_ref[...], total, ((1,), (1,)))
     for c in range(ways_col):
@@ -130,7 +132,8 @@
         out_ref[r] = diag
 
 
-def last(parts_ref, out_ref):
+def last(parts_ref, grad_ref, out_ref, grad_out_ref):
+    grad_out_ref[...] = grad_ref[...]
     total = parts_ref[0]
     for r in range(1, parts_ref.shape[0]):
         total = total + parts_ref[r]
@@ -161,16 +164,16 @@
     parts, panel_rows = pl.pallas_call(
         multiply,
         out_shape=[like(X_WAYS, width, quarter), like(width, quarter)],
-        in_specs=[vmem] * 5,
+        in_specs=[vmem] * 4,
         out_specs=[vmem] * 2,
         scratch_shapes=[pltpu.VMEM((width, cols), F32)],
         compiler_params=pltpu.CompilerParams(vmem_limit_bytes=48 << 20),
-    )(pair, got, trail_adjoint, panel_adjoint.T, inv_diag)
-    both = call(gram, like(ways_col, thin_cols, quarter + width), exchange(parts, "col", groups), panel_rows)
+    )(pair, got, trail_adjoint, panel_adjoint.T)
+    both = call(gram, like(ways_col, thin_cols, quarter + width), exchange(parts, "col", groups), panel_rows, inv_diag)
     grad, mine = call(
         finish, [like(thin_cols, rows_here), like(ways_row, thin_cols, width)], exchange(both, "col")
     )
-    diag = call(last, like(thin_cols, width), exchange(mine, "row"))
+    diag, grad = call(last, [like(thin_cols, width), like(thin_cols, rows_here)], exchange(mine, "row"), grad)
     return (grad.T, diag.T)
 
 

time: 89.5 us -> 88 us (0.983)
  no operation moved by 1% of the time
where the time goes in v4:
time: 88 us; the launch traced here: 87.6 us
  blocking collectives  83.1 us (94%)
  Pallas kernels  2.36 us (3%)
  between operations  1.47 us (2%)
    all_to_all x5, blocking collectives, exchange(): lax.all_to_all(value, axis, split_axis=0, concat_axis=0, axis_index_group...  79.5 us
    all_gather x1, blocking collectives, body(): pair = lax.all_gather(got, 'row', axis=0, axis_index_groups=chips)  3.52 us

profile of v4, /device:TPU:1, one launch (start us, length us, event | category | flops | bytes accessed | tf_op | source)
XLA Modules:
  0.0 87.6 jit_solution(5924485401752199672)
XLA Ops:
  0.6 0.0 copy-start
  1.4 0.0 copy-start.2
  1.4 0.7 copy-done.2
  2.2 0.0 copy-start.3
  2.2 20.8 %all_to_all.25.every_ref = f32[16,4,512]{2,1,0:T(4,128)S(1)} all-to-all(f32[16,4,512]{2,1,0:T(4,128)S(1)} %shard_map.68), channel_id=1, replica_groups=mesh['row'=16,'col'=32] {'row'}, dimensions={0} | all-to-all | bytes 262144 | tf_op jit(solution)/shard_map/all_to_all | solution.py:14
  23.0 20.2 %all_to_all.26.got_ref = f32[32,4,512]{2,1,0:T(4,128)S(1)} all-to-all(f32[32,4,512]{2,1,0:T(4,128)S(1)} %shard_map.69), channel_id=1, replica_groups=mesh['row'=16,'col'=32] {'col'}, dimensions={0} | all-to-all | bytes 524288 | tf_op jit(solution)/shard_map/all_to_all | solution.py:14
  43.2 3.5 %all-gather = f32[64,4,512]{2,1,0:T(4,128)S(1)} all-gather(f32[32,4,512]{2,1,0:T(4,128)S(1)} %all_to_all.26.got_ref), channel_id=2, replica_groups={{0,32},{64,96},{128,160},{192,224},{256,288},{320,352},{384,416},{448,4..., dimensions={0}, use_global_device_ids=true | all-gather | bytes 786432 | tf_op jit(solution)/shard_map/all_gather | solution.py:162
  46.7 0.0 copy-start.1
  46.7 0.0 copy-done
  46.7 0.0 copy-done.3
  46.7 1.2 %shard_map.70 = (f32[4,128,256]{2,1,0:T(8,128)S(1)}, f32[128,256]{1,0:T(8,128)S(1)}) custom-call(f32[2,32,4,512]{3,2,1,0:T(4,128)S(1)} %bitcast.5, f32[32,4,512]{2,1,0:T(4,128)S(1)} %all_to_all.26.got_ref, f32[1024,512]{1,0:T(8,128)S(1)} %copy-done, f32[4,1024]{1,0:T(4,128)S(1)} %bitcast.8), custom_call_target="tpu_custom_call" | custom-call | tf_op jit(solution)/shard_map/pallas_call | solution.py:164
  47.9 11.7 %all_to_all.27.parts_ref = f32[4,128,256]{2,1,0:T(8,128)S(1)} all-to-all(f32[4,128,256]{2,1,0:T(8,128)S(1)} %get-tuple-element.8), channel_id=1, replica_groups={{0,8,16,24},{1,9,17,25},{2,10,18,26},{3,11,19,27},{4,12,20,28},{5,13,21..., dimensions={0} | all-to-all | bytes 1048576 | tf_op jit(solution)/shard_map/all_to_all | solution.py:14
  59.6 0.0 copy-done.1
  59.6 0.5 shard_map.71
  60.1 14.0 %all_to_all.28.parts_ref = f32[32,4,384]{2,1,0:T(4,128)S(1)} all-to-all(f32[32,4,384]{2,1,0:T(4,128)S(1)} %shard_map.71), channel_id=1, replica_groups=mesh['row'=16,'col'=32] {'col'}, dimensions={0} | all-to-all | bytes 393216 | tf_op jit(solution)/shard_map/all_to_all | solution.py:14
  74.2 12.8 %all_to_all.29.parts_ref = f32[16,4,128]{2,1,0:T(4,128)S(1)} all-to-all(f32[16,4,128]{2,1,0:T(4,128)S(1)} %get-tuple-element.10), channel_id=1, replica_groups=mesh['row'=16,'col'=32] {'row'}, dimensions={0} | all-to-all | bytes 65536 | tf_op jit(solution)/shard_map/all_to_all | solution.py:14
  87.0 0.6 shard_map.73
  (3 shorter events, 0.1 us)
Async XLA Ops:
  0.6 46.1 %copy-start = (f32[1024,512]{1,0:T(8,128)S(1)}, f32[1024,512]{1,0:T(8,128)}, u32[]{:S(2)}) copy-start(f32[1024,512]{1,0:T(8,128)} %trail_ref.1) | copy-start | bytes 6291460
  1.4 0.7 copy-start.2
  2.2 44.5 %copy-start.3 = (f32[1024,4]{0,1:T(4,128)S(1)}, f32[1024,4]{0,1:T(4,128)}, u32[]{:S(2)}) copy-start(f32[1024,4]{0,1:T(4,128)} %param.7) | copy-start | bytes 49156
  46.7 12.9 %copy-start.1 = (f32[128,128]{1,0:T(8,128)S(1)}, f32[128,128]{1,0:T(8,128)}, u32[]{:S(2)}) copy-start(f32[128,128]{1,0:T(8,128)} %inv_ref.1) | copy-start | bytes 196612

commit v5 on v4

--- a/solution.py
+++ b/solution.py
@@ -5,9 +5,16 @@
 from jax.experimental.pallas import tpu as pltpu
 from jax.sharding import PartitionSpec as P
 
-X_WAYS = 4
+Y_WAYS = 8
+BLOCK_X, BLOCK_Y = 4, 2
+BLOCK = BLOCK_X * BLOCK_Y
 CORES = 2
 F32 = jnp.float32
+
+
+def place(col):
+    x, y = col // Y_WAYS, col % Y_WAYS
+    return x % BLOCK_X * BLOCK_Y + y % BLOCK_Y
 
 
 def exchange(value, axis, groups=None):
@@ -71,13 +78,13 @@
 def route(every_ref, thin_ref, out_ref):
     ways_row = every_ref.shape[0]
     ways_col = out_ref.shape[0]
-    quarter = thin_ref.shape[1] // X_WAYS
-    share = out_ref.shape[2] - quarter
+    part = thin_ref.shape[1] // BLOCK
+    share = out_ref.shape[2] - part
     for c in range(ways_col):
         p = c // ways_row
-        x = c // (ways_col // X_WAYS)
+        x = place(c)
         out_ref[c, :, :share] = every_ref[c % ways_row, :, p * share : (p + 1) * share]
-        out_ref[c, :, share:] = thin_ref[:, x * quarter : (x + 1) * quarter]
+        out_ref[c, :, share:] = thin_ref[:, x * part : (x + 1) * part]
 
 
 def multiply(pair_ref, got_ref, trail_ref, adjoint_ref, out_ref, panel_ref, work_ref):
@@ -93,10 +100,10 @@
     per_eight = 8 // thin_cols
     col = lax.axis_index("col")
     eight = pl.ds(pl.multiple_of(col // per_eight * 8, 8), 8)
-    owner = lax.broadcasted_iota(jnp.int32, (8, rows_here // X_WAYS), 0) // thin_cols
-    quarter = rows_here // X_WAYS
-    for x in range(X_WAYS):
-        at = slice(x * quarter, (x + 1) * quarter)
+    owner = lax.broadcasted_iota(jnp.int32, (8, rows_here // BLOCK), 0) // thin_cols
+    part = rows_here // BLOCK
+    for x in range(BLOCK):
+        at = slice(x * part, (x + 1) * part)
         out_ref[x] = dot(scaled, trail_ref[at, :], ((1,), (1,)))
         added = jnp.concatenate([adjoint_ref[:, at]] * per_eight, axis=0)
         added = jnp.where(owner == lax.rem(col, per_eight), added, jnp.zeros_like(added))
@@ -106,28 +113,28 @@
 def gram(parts_ref, panel_ref, inv_ref, out_ref):
     ways_col, thin_cols, _ = out_ref.shape
     total = parts_ref[0]
-    for x in range(1, X_WAYS):
+    for x in range(1, BLOCK):
         total = total + parts_ref[x]
     total = dot(inv_ref[...].T, total, ((1,), (0,)))
-    quarter = total.shape[1]
+    part = total.shape[1]
     diag = dot(-panel_ref[...], total, ((1,), (1,)))
     for c in range(ways_col):
         at = slice(c * thin_cols, (c + 1) * thin_cols)
-        out_ref[c, :, :quarter] = total[at, :]
-        out_ref[c, :, quarter:] = diag[at, :]
+        out_ref[c, :, :part] = total[at, :]
+        out_ref[c, :, part:] = diag[at, :]
 
 
 def finish(parts_ref, grad_ref, out_ref):
     ways_col = parts_ref.shape[0]
-    y_ways = ways_col // X_WAYS
-    quarter = grad_ref.shape[1] // X_WAYS
+    part = grad_ref.shape[1] // BLOCK
     diag = None
-    for x in range(X_WAYS):
-        total = parts_ref[x * y_ways]
-        for y in range(1, y_ways):
-            total = total + parts_ref[x * y_ways + y]
-        grad_ref[:, x * quarter : (x + 1) * quarter] = total[:, :quarter]
-        diag = total[:, quarter:] if diag is None else diag + total[:, quarter:]
+    for i in range(BLOCK):
+        total = None
+        for c in range(ways_col):
+            if place(c) == i:
+                total = parts_ref[c] if total is None else total + parts_ref[c]
+        grad_ref[:, i * part : (i + 1) * part] = total[:, :part]
+        diag = total[:, part:] if diag is None else diag + total[:, part:]
     for r in range(out_ref.shape[0]):
         out_ref[r] = diag
 
@@ -146,9 +153,12 @@
     ways_row = lax.axis_size("row")
     ways_col = lax.axis_size("col")
     cols = trail_adjoint.shape[1]
-    quarter = rows_here // X_WAYS
-    y_ways = ways_col // X_WAYS
-    groups = [[x * y_ways + y for x in range(X_WAYS)] for y in range(y_ways)]
+    part = rows_here // BLOCK
+    groups = {}
+    for c in range(ways_col):
+        block = (c // Y_WAYS // BLOCK_X, c % Y_WAYS // BLOCK_Y)
+        groups.setdefault(block, []).append(c)
+    groups = [sorted(g, key=place) for g in groups.values()]
     thin = panel.T
 
     def spreading(*refs):
@@ -156,20 +166,20 @@
 
     share = cols // CORES
     copies = call(spreading, like(ways_row, thin_cols, rows_here // CORES), panel_index, thin, scalars=1)
-    sent = call(route, like(ways_col, thin_cols, share + quarter), exchange(copies, "row"), thin)
+    sent = call(route, like(ways_col, thin_cols, share + part), exchange(copies, "row"), thin)
     got = exchange(sent, "col")
     chips = [list(range(r, r + CORES)) for r in range(0, ways_row, CORES)]
-    pair = lax.all_gather(got, "row", axis=0, axis_index_groups=chips)
+    pair = lax.all_gather(jnp.concatenate([got, got[:, :, :128]], axis=2), "row", axis=0, axis_index_groups=chips)
     vmem = pl.BlockSpec(memory_space=pltpu.VMEM)
     parts, panel_rows = pl.pallas_call(
         multiply,
-        out_shape=[like(X_WAYS, width, quarter), like(width, quarter)],
+        out_shape=[like(BLOCK, width, part), like(width, part)],
         in_specs=[vmem] * 4,
         out_specs=[vmem] * 2,
         scratch_shapes=[pltpu.VMEM((width, cols), F32)],
         compiler_params=pltpu.CompilerParams(vmem_limit_bytes=48 << 20),
     )(pair, got, trail_adjoint, panel_adjoint.T)
-    both = call(gram, like(ways_col, thin_cols, quarter + width), exchange(parts, "col", groups), panel_rows, inv_diag)
+    both = call(gram, like(ways_col, thin_cols, part + width), exchange(parts, "col", groups), panel_rows, inv_diag)
     grad, mine = call(
         finish, [like(thin_cols, rows_here), like(ways_row, thin_cols, width)], exchange(both, "col")
     )

time: 88 us -> 86.8 us (0.986)
  blocking collectives: 83.1 us -> 82 us
    all_to_all x5, blocking collectives: 79.5 us -> 78.5 us  [exchange(): lax.all_to_all(value, axis, split_axis=0, concat_axis=0, axis_index_group...]
where the time goes in v5:
time: 86.8 us; the launch traced here: 86.4 us
  blocking collectives  82 us (94%)
  Pallas kernels  2.13 us (2%)
  between operations  1.48 us (2%)
    all_to_all x5, blocking collectives, exchange(): lax.all_to_all(value, axis, split_axis=0, concat_axis=0, axis_index_group...  78.5 us
    all_gather x1, blocking collectives, body(): lax.all_gather(jnp.concatenate([got, got[:, :, :128]], axis=2), 'row', ax...  3.45 us

profile of v5, /device:TPU:1, one launch (start us, length us, event | category | flops | bytes accessed | tf_op | source)
XLA Modules:
  0.0 86.4 jit_solution(1080345568395257153)
XLA Ops:
  0.6 0.0 copy-start
  1.4 0.0 copy-start.2
  1.4 0.7 copy-done.2
  2.2 0.0 copy-start.3
  2.2 20.8 %all_to_all.25.every_ref = f32[16,4,512]{2,1,0:T(4,128)S(1)} all-to-all(f32[16,4,512]{2,1,0:T(4,128)S(1)} %shard_map.68), channel_id=1, replica_groups=mesh['row'=16,'col'=32] {'row'}, dimensions={0} | all-to-all | bytes 262144 | tf_op jit(solution)/shard_map/all_to_all | solution.py:21
  23.0 19.4 %all_to_all.26.got_ref = f32[32,4,384]{2,1,0:T(4,128)S(1)} all-to-all(f32[32,4,384]{2,1,0:T(4,128)S(1)} %shard_map.69), channel_id=1, replica_groups=mesh['row'=16,'col'=32] {'col'}, dimensions={0} | all-to-all | bytes 393216 | tf_op jit(solution)/shard_map/all_to_all | solution.py:21
  42.4 0.1 pad_maximum_fusion
  42.5 3.4 %all-gather = f32[64,4,512]{2,1,0:T(4,128)S(1)} all-gather(f32[32,4,512]{2,1,0:T(4,128)S(1)} %pad_maximum_fusion), channel_id=2, replica_groups={{0,32},{64,96},{128,160},{192,224},{256,288},{320,352},{384,416},{448,4..., dimensions={0}, use_global_device_ids=true | all-gather | bytes 786432 | tf_op jit(solution)/shard_map/all_gather | solution.py:172
  46.0 0.0 copy-start.1
  46.0 0.0 copy-done
  46.0 0.0 copy-done.3
  46.0 1.0 %shard_map.70 = (f32[8,128,128]{2,1,0:T(8,128)S(1)}, f32[128,128]{1,0:T(8,128)S(1)}) custom-call(f32[2,32,4,512]{3,2,1,0:T(4,128)S(1)} %bitcast.5, f32[32,4,384]{2,1,0:T(4,128)S(1)} %all_to_all.26.got_ref, f32[1024,512]{1,0:T(8,128)S(1)} %copy-done, f32[4,1024]{1,0:T(4,128)S(1)} %bitcast.8), custom_call_target="tpu_custom_call" | custom-call | tf_op jit(solution)/shard_map/pallas_call | solution.py:174
  47.0 12.9 %all_to_all.27.parts_ref = f32[8,128,128]{2,1,0:T(8,128)S(1)} all-to-all(f32[8,128,128]{2,1,0:T(8,128)S(1)} %get-tuple-element.8), channel_id=1, replica_groups={{0,1,8,9,16,17,24,25},{2,3,10,11,18,19,26,27},{4,5,12,13,20,21,28,29},{..., dimensions={0} | all-to-all | bytes 1048576 | tf_op jit(solution)/shard_map/all_to_all | solution.py:21
  59.9 0.0 copy-done.1
  59.9 0.4 shard_map.71
  60.3 13.0 %all_to_all.28.parts_ref = f32[32,4,256]{2,1,0:T(4,128)S(1)} all-to-all(f32[32,4,256]{2,1,0:T(4,128)S(1)} %shard_map.71), channel_id=1, replica_groups=mesh['row'=16,'col'=32] {'col'}, dimensions={0} | all-to-all | bytes 262144 | tf_op jit(solution)/shard_map/all_to_all | solution.py:21
  73.4 12.4 %all_to_all.29.parts_ref = f32[16,4,128]{2,1,0:T(4,128)S(1)} all-to-all(f32[16,4,128]{2,1,0:T(4,128)S(1)} %get-tuple-element.10), channel_id=1, replica_groups=mesh['row'=16,'col'=32] {'row'}, dimensions={0} | all-to-all | bytes 65536 | tf_op jit(solution)/shard_map/all_to_all | solution.py:21
  85.8 0.6 shard_map.73
  (4 shorter events, 0.1 us)
Async XLA Ops:
  0.6 45.3 %copy-start = (f32[1024,512]{1,0:T(8,128)S(1)}, f32[1024,512]{1,0:T(8,128)}, u32[]{:S(2)}) copy-start(f32[1024,512]{1,0:T(8,128)} %trail_ref.1) | copy-start | bytes 6291460
  1.4 0.7 copy-start.2
  2.2 43.8 %copy-start.3 = (f32[1024,4]{0,1:T(4,128)S(1)}, f32[1024,4]{0,1:T(4,128)}, u32[]{:S(2)}) copy-start(f32[1024,4]{0,1:T(4,128)} %param.7) | copy-start | bytes 49156
  46.0 13.9 %copy-start.1 = (f32[128,128]{1,0:T(8,128)S(1)}, f32[128,128]{1,0:T(8,128)}, u32[]{:S(2)}) copy-start(f32[128,128]{1,0:T(8,128)} %inv_ref.1) | copy-start | bytes 196612

commit v6 on v5

--- a/solution.py
+++ b/solution.py
@@ -12,6 +12,11 @@
 F32 = jnp.float32
 
 
+def order(ways):
+    stride = 5 if ways > 16 else 5
+    return [stride * i % ways for i in range(ways)]
+
+
 def place(col):
     x, y = col // Y_WAYS, col % Y_WAYS
     return x % BLOCK_X * BLOCK_Y + y % BLOCK_Y
@@ -34,7 +39,9 @@
     def one(p, q):
         return lax.dot_general(p, q, (contract, ((), ())), preferred_element_type=F32)
 
-    return one(a_high, b_high) + (one(a_high, b_low) + one(a_low, b_high))
+    rows = a.shape[0]
+    both = one(jnp.concatenate([a_high, a_low], axis=0), b_high)
+    return both[:rows] + (one(a_high, b_low) + both[rows:])
 
 
 def call(kernel, shapes, *args, scalars=0):
@@ -71,8 +78,9 @@
             for i in range(1, ratio):
                 piece = jnp.where(offset == i, thin_ref[:, at + i * width : at + (i + 1) * width], piece)
             to = p * share + j % blocks * width
-            for r in range(j // blocks, ways_row, CORES):
-                out_ref[r, :, to : to + width] = piece
+            for i, r in enumerate(order(ways_row)):
+                if r % CORES == j // blocks:
+                    out_ref[i, :, to : to + width] = piece
 
 
 def route(every_ref, thin_ref, out_ref):
@@ -80,31 +88,33 @@
     ways_col = out_ref.shape[0]
     part = thin_ref.shape[1] // BLOCK
     share = out_ref.shape[2] - part
-    for c in range(ways_col):
+    for i, c in enumerate(order(ways_col)):
         p = c // ways_row
+        source = order(ways_row).index(c % ways_row)
         x = place(c)
-        out_ref[c, :, :share] = every_ref[c % ways_row, :, p * share : (p + 1) * share]
-        out_ref[c, :, share:] = thin_ref[:, x * part : (x + 1) * part]
+        out_ref[i, :, :share] = every_ref[source, :, p * share : (p + 1) * share]
+        out_ref[i, :, share:] = thin_ref[:, x * part : (x + 1) * part]
 
 
 def multiply(pair_ref, got_ref, trail_ref, adjoint_ref, out_ref, panel_ref, work_ref):
     ways_col, thin_cols, _ = got_ref.shape
     rows_here, cols = trail_ref.shape
     share = cols // CORES
-    for c in range(ways_col):
+    for i, c in enumerate(order(ways_col)):
         at = slice(c * thin_cols, (c + 1) * thin_cols)
         for core in range(CORES):
-            work_ref[at, core * share : (core + 1) * share] = pair_ref[core, c, :, :share]
-        panel_ref[at, :] = got_ref[c, :, share:]
+            work_ref[at, core * share : (core + 1) * share] = pair_ref[core, i, :, :share]
+        panel_ref[at, :] = got_ref[i, :, share:]
     scaled = work_ref[...] * -2.0
     per_eight = 8 // thin_cols
     col = lax.axis_index("col")
     eight = pl.ds(pl.multiple_of(col // per_eight * 8, 8), 8)
     owner = lax.broadcasted_iota(jnp.int32, (8, rows_here // BLOCK), 0) // thin_cols
     part = rows_here // BLOCK
+    product = dot(scaled, trail_ref[...], ((1,), (1,)))
     for x in range(BLOCK):
         at = slice(x * part, (x + 1) * part)
-        out_ref[x] = dot(scaled, trail_ref[at, :], ((1,), (1,)))
+        out_ref[x] = product[:, at]
         added = jnp.concatenate([adjoint_ref[:, at]] * per_eight, axis=0)
         added = jnp.where(owner == lax.rem(col, per_eight), added, jnp.zeros_like(added))
         out_ref[x, eight, :] = out_ref[x, eight, :] + added
@@ -118,10 +128,10 @@
     total = dot(inv_ref[...].T, total, ((1,), (0,)))
     part = total.shape[1]
     diag = dot(-panel_ref[...], total, ((1,), (1,)))
-    for c in range(ways_col):
+    for i, c in enumerate(order(ways_col)):
         at = slice(c * thin_cols, (c + 1) * thin_cols)
-        out_ref[c, :, :part] = total[at, :]
-        out_ref[c, :, part:] = diag[at, :]
+        out_ref[i, :, :part] = total[at, :]
+        out_ref[i, :, part:] = diag[at, :]
 
 
 def finish(parts_ref, grad_ref, out_ref):
@@ -130,9 +140,9 @@
     diag = None
     for i in range(BLOCK):
         total = None
-        for c in range(ways_col):
+        for j, c in enumerate(order(ways_col)):
             if place(c) == i:
-                total = parts_ref[c] if total is None else total + parts_ref[c]
+                total = parts_ref[j] if total is None else total + parts_ref[j]
         grad_ref[:, i * part : (i + 1) * part] = total[:, :part]
         diag = total[:, part:] if diag is None else diag + total[:, part:]
     for r in range(out_ref.shape[0]):
@@ -154,6 +164,7 @@
     ways_col = lax.axis_size("col")
     cols = trail_adjoint.shape[1]
     part = rows_here // BLOCK
+    rows, columns = [order(ways_row)], [order(ways_col)]
     groups = {}
     for c in range(ways_col):
         block = (c // Y_WAYS // BLOCK_X, c % Y_WAYS // BLOCK_Y)
@@ -166,8 +177,8 @@
 
     share = cols // CORES
     copies = call(spreading, like(ways_row, thin_cols, rows_here // CORES), panel_index, thin, scalars=1)
-    sent = call(route, like(ways_col, thin_cols, share + part), exchange(copies, "row"), thin)
-    got = exchange(sent, "col")
+    sent = call(route, like(ways_col, thin_cols, share + part), exchange(copies, "row", rows), thin)
+    got = exchange(sent, "col", columns)
     chips = [list(range(r, r + CORES)) for r in range(0, ways_row, CORES)]
     pair = lax.all_gather(jnp.concatenate([got, got[:, :, :128]], axis=2), "row", axis=0, axis_index_groups=chips)
     vmem = pl.BlockSpec(memory_space=pltpu.VMEM)
@@ -181,9 +192,9 @@
     )(pair, got, trail_adjoint, panel_adjoint.T)
     both = call(gram, like(ways_col, thin_cols, part + width), exchange(parts, "col", groups), panel_rows, inv_diag)
     grad, mine = call(
-        finish, [like(thin_cols, rows_here), like(ways_row, thin_cols, width)], exchange(both, "col")
+        finish, [like(thin_cols, rows_here), like(ways_row, thin_cols, width)], exchange(both, "col", columns)
     )
-    diag, grad = call(last, [like(thin_cols, width), like(thin_cols, rows_here)], exchange(mine, "row"), grad)
+    diag, grad = call(last, [like(thin_cols, width), like(thin_cols, rows_here)], exchange(mine, "row", rows), grad)
     return (grad.T, diag.T)
 
 

time: 86.8 us -> 86.2 us (level)
    all_to_all x5, blocking collectives: 78.5 us -> 77.6 us  [exchange(): lax.all_to_all(value, axis, split_axis=0, concat_axis=0, axis_index_group...]
where the time goes in v6:
time: 86.2 us; the launch traced here: 85.8 us
  blocking collectives  81.6 us (95%)
  Pallas kernels  1.9 us (2%)
  between operations  1.48 us (2%)
    all_to_all x5, blocking collectives, exchange(): lax.all_to_all(value, axis, split_axis=0, concat_axis=0, axis_index_group...  77.6 us
    all_gather x1, blocking collectives, body(): lax.all_gather(jnp.concatenate([got, got[:, :, :128]], axis=2), 'row', ax...  4.06 us

profile of v6, /device:TPU:1, one launch (start us, length us, event | category | flops | bytes accessed | tf_op | source)
XLA Modules:
  0.0 85.8 jit_solution(3347423104011427147)
XLA Ops:
  0.6 0.0 copy-start
  1.4 0.0 copy-start.2
  1.4 0.7 copy-done.2
  2.2 0.0 copy-start.3
  2.2 20.4 %all_to_all.25.every_ref = f32[16,4,512]{2,1,0:T(4,128)S(1)} all-to-all(f32[16,4,512]{2,1,0:T(4,128)S(1)} %shard_map.68), channel_id=1, replica_groups={{0,160,320,480,128,288,448,96,256,416,64,224,384,32,192,352},{1,161,321..., dimensions={0} | all-to-all | bytes 262144 | tf_op jit(solution)/shard_map/all_to_all | solution.py:26
  22.6 19.4 %all_to_all.26.got_ref = f32[32,4,384]{2,1,0:T(4,128)S(1)} all-to-all(f32[32,4,384]{2,1,0:T(4,128)S(1)} %shard_map.69), channel_id=1, replica_groups={{0,5,10,15,20,25,30,3,8,13,18,23,28,1,6,11,16,21,26,31,4,9,14,19,24,29,..., dimensions={0} | all-to-all | bytes 393216 | tf_op jit(solution)/shard_map/all_to_all | solution.py:26
  42.0 0.1 pad_maximum_fusion
  42.1 4.1 %all-gather = f32[64,4,512]{2,1,0:T(4,128)S(1)} all-gather(f32[32,4,512]{2,1,0:T(4,128)S(1)} %pad_maximum_fusion), channel_id=2, replica_groups={{0,32},{64,96},{128,160},{192,224},{256,288},{320,352},{384,416},{448,4..., dimensions={0}, use_global_device_ids=true | all-gather | bytes 786432 | tf_op jit(solution)/shard_map/all_gather | solution.py:183
  46.2 0.0 copy-start.1
  46.2 0.0 copy-done
  46.2 0.0 copy-done.3
  46.2 0.8 shard_map.70
  47.0 12.4 %all_to_all.27.parts_ref = f32[8,128,128]{2,1,0:T(8,128)S(1)} all-to-all(f32[8,128,128]{2,1,0:T(8,128)S(1)} %get-tuple-element.8), channel_id=1, replica_groups={{0,1,8,9,16,17,24,25},{2,3,10,11,18,19,26,27},{4,5,12,13,20,21,28,29},{..., dimensions={0} | all-to-all | bytes 1048576 | tf_op jit(solution)/shard_map/all_to_all | solution.py:26
  59.4 0.0 copy-done.1
  59.4 0.4 shard_map.71
  59.8 12.8 %all_to_all.28.parts_ref = f32[32,4,256]{2,1,0:T(4,128)S(1)} all-to-all(f32[32,4,256]{2,1,0:T(4,128)S(1)} %shard_map.71), channel_id=1, replica_groups={{0,5,10,15,20,25,30,3,8,13,18,23,28,1,6,11,16,21,26,31,4,9,14,19,24,29,..., dimensions={0} | all-to-all | bytes 262144 | tf_op jit(solution)/shard_map/all_to_all | solution.py:26
  72.6 12.6 %all_to_all.29.parts_ref = f32[16,4,128]{2,1,0:T(4,128)S(1)} all-to-all(f32[16,4,128]{2,1,0:T(4,128)S(1)} %get-tuple-element.10), channel_id=1, replica_groups={{0,160,320,480,128,288,448,96,256,416,64,224,384,32,192,352},{1,161,321..., dimensions={0} | all-to-all | bytes 65536 | tf_op jit(solution)/shard_map/all_to_all | solution.py:26
  85.2 0.6 shard_map.73
  (4 shorter events, 0.1 us)
Async XLA Ops:
  0.6 45.5 %copy-start = (f32[1024,512]{1,0:T(8,128)S(1)}, f32[1024,512]{1,0:T(8,128)}, u32[]{:S(2)}) copy-start(f32[1024,512]{1,0:T(8,128)} %trail_ref.1) | copy-start | bytes 6291460
  1.4 0.7 copy-start.2
  2.2 44.0 %copy-start.3 = (f32[1024,4]{0,1:T(4,128)S(1)}, f32[1024,4]{0,1:T(4,128)}, u32[]{:S(2)}) copy-start(f32[1024,4]{0,1:T(4,128)} %param.7) | copy-start | bytes 49156
  46.2 13.2 %copy-start.1 = (f32[128,128]{1,0:T(8,128)S(1)}, f32[128,128]{1,0:T(8,128)}, u32[]{:S(2)}) copy-start(f32[128,128]{1,0:T(8,128)} %inv_ref.1) | copy-start | bytes 196612

commit v7 on v6

--- a/solution.py
+++ b/solution.py
@@ -19,7 +19,7 @@
 
 def place(col):
     x, y = col // Y_WAYS, col % Y_WAYS
-    return x % BLOCK_X * BLOCK_Y + y % BLOCK_Y
+    return y % BLOCK_Y * BLOCK_X + x % BLOCK_X
 
 
 def exchange(value, axis, groups=None):

time: 86.2 us -> 86 us (level)
  no operation moved by 1% of the time
where the time goes in v7:
time: 86 us; the launch traced here: 85.6 us
  blocking collectives  81.4 us (95%)
  Pallas kernels  1.9 us (2%)
  between operations  1.48 us (2%)
    all_to_all x5, blocking collectives, exchange(): lax.all_to_all(value, axis, split_axis=0, concat_axis=0, axis_index_group...  77.4 us
    all_gather x1, blocking collectives, body(): lax.all_gather(jnp.concatenate([got, got[:, :, :128]], axis=2), 'row', ax...  4.06 us

profile of v7, /device:TPU:1, one launch (start us, length us, event | category | flops | bytes accessed | tf_op | source)
XLA Modules:
  0.0 85.6 jit_solution(13683253963196615235)
XLA Ops:
  0.6 0.0 copy-start
  1.4 0.0 copy-start.2
  1.4 0.7 copy-done.2
  2.2 0.0 copy-start.3
  2.2 20.4 %all_to_all.25.every_ref = f32[16,4,512]{2,1,0:T(4,128)S(1)} all-to-all(f32[16,4,512]{2,1,0:T(4,128)S(1)} %shard_map.68), channel_id=1, replica_groups={{0,160,320,480,128,288,448,96,256,416,64,224,384,32,192,352},{1,161,321..., dimensions={0} | all-to-all | bytes 262144 | tf_op jit(solution)/shard_map/all_to_all | solution.py:26
  22.6 19.4 %all_to_all.26.got_ref = f32[32,4,384]{2,1,0:T(4,128)S(1)} all-to-all(f32[32,4,384]{2,1,0:T(4,128)S(1)} %shard_map.69), channel_id=1, replica_groups={{0,5,10,15,20,25,30,3,8,13,18,23,28,1,6,11,16,21,26,31,4,9,14,19,24,29,..., dimensions={0} | all-to-all | bytes 393216 | tf_op jit(solution)/shard_map/all_to_all | solution.py:26
  42.0 0.1 pad_maximum_fusion
  42.1 4.1 %all-gather = f32[64,4,512]{2,1,0:T(4,128)S(1)} all-gather(f32[32,4,512]{2,1,0:T(4,128)S(1)} %pad_maximum_fusion), channel_id=2, replica_groups={{0,32},{64,96},{128,160},{192,224},{256,288},{320,352},{384,416},{448,4..., dimensions={0}, use_global_device_ids=true | all-gather | bytes 786432 | tf_op jit(solution)/shard_map/all_gather | solution.py:183
  46.2 0.0 copy-start.1
  46.2 0.0 copy-done
  46.2 0.0 copy-done.3
  46.2 0.8 shard_map.70
  47.0 12.0 %all_to_all.27.parts_ref = f32[8,128,128]{2,1,0:T(8,128)S(1)} all-to-all(f32[8,128,128]{2,1,0:T(8,128)S(1)} %get-tuple-element.8), channel_id=1, replica_groups={{0,8,16,24,1,9,17,25},{2,10,18,26,3,11,19,27},{4,12,20,28,5,13,21,29},{..., dimensions={0} | all-to-all | bytes 1048576 | tf_op jit(solution)/shard_map/all_to_all | solution.py:26
  59.0 0.0 copy-done.1
  59.0 0.4 shard_map.71
  59.4 13.2 %all_to_all.28.parts_ref = f32[32,4,256]{2,1,0:T(4,128)S(1)} all-to-all(f32[32,4,256]{2,1,0:T(4,128)S(1)} %shard_map.71), channel_id=1, replica_groups={{0,5,10,15,20,25,30,3,8,13,18,23,28,1,6,11,16,21,26,31,4,9,14,19,24,29,..., dimensions={0} | all-to-all | bytes 262144 | tf_op jit(solution)/shard_map/all_to_all | solution.py:26
  72.7 12.4 %all_to_all.29.parts_ref = f32[16,4,128]{2,1,0:T(4,128)S(1)} all-to-all(f32[16,4,128]{2,1,0:T(4,128)S(1)} %get-tuple-element.10), channel_id=1, replica_groups={{0,160,320,480,128,288,448,96,256,416,64,224,384,32,192,352},{1,161,321..., dimensions={0} | all-to-all | bytes 65536 | tf_op jit(solution)/shard_map/all_to_all | solution.py:26
  85.0 0.6 shard_map.73
  (4 shorter events, 0.1 us)
Async XLA Ops:
  0.6 45.5 %copy-start = (f32[1024,512]{1,0:T(8,128)S(1)}, f32[1024,512]{1,0:T(8,128)}, u32[]{:S(2)}) copy-start(f32[1024,512]{1,0:T(8,128)} %trail_ref.1) | copy-start | bytes 6291460
  1.4 0.7 copy-start.2
  2.2 44.0 %copy-start.3 = (f32[1024,4]{0,1:T(4,128)S(1)}, f32[1024,4]{0,1:T(4,128)}, u32[]{:S(2)}) copy-start(f32[1024,4]{0,1:T(4,128)} %param.7) | copy-start | bytes 49156
  46.2 12.8 %copy-start.1 = (f32[128,128]{1,0:T(8,128)S(1)}, f32[128,128]{1,0:T(8,128)}, u32[]{:S(2)}) copy-start(f32[128,128]{1,0:T(8,128)} %inv_ref.1) | copy-start | bytes 196612

commit v8 on v7

--- a/solution.py
+++ b/solution.py
@@ -13,7 +13,7 @@
 
 
 def order(ways):
-    stride = 5 if ways > 16 else 5
+    stride = 5 if ways > 16 else 3
     return [stride * i % ways for i in range(ways)]
 
 

time: 86 us -> 85.7 us (level)
  no operation moved by 1% of the time
where the time goes in v8:
time: 85.7 us; the launch traced here: 85.3 us
  blocking collectives  81.2 us (95%)
  Pallas kernels  1.9 us (2%)
  between operations  1.48 us (2%)
    all_to_all x5, blocking collectives, exchange(): lax.all_to_all(value, axis, split_axis=0, concat_axis=0, axis_index_group...  77 us
    all_gather x1, blocking collectives, body(): lax.all_gather(jnp.concatenate([got, got[:, :, :128]], axis=2), 'row', ax...  4.19 us

profile of v8, /device:TPU:1, one launch (start us, length us, event | category | flops | bytes accessed | tf_op | source)
XLA Modules:
  0.0 85.3 jit_solution(7169343100292296903)
XLA Ops:
  0.6 0.0 copy-start
  1.4 0.0 copy-start.2
  1.4 0.7 copy-done.2
  2.2 0.0 copy-start.3
  2.2 20.0 %all_to_all.25.every_ref = f32[16,4,512]{2,1,0:T(4,128)S(1)} all-to-all(f32[16,4,512]{2,1,0:T(4,128)S(1)} %shard_map.68), channel_id=1, replica_groups={{0,96,192,288,384,480,64,160,256,352,448,32,128,224,320,416},{1,97,193,..., dimensions={0} | all-to-all | bytes 262144 | tf_op jit(solution)/shard_map/all_to_all | solution.py:26
  22.2 19.3 %all_to_all.26.got_ref = f32[32,4,384]{2,1,0:T(4,128)S(1)} all-to-all(f32[32,4,384]{2,1,0:T(4,128)S(1)} %shard_map.69), channel_id=1, replica_groups={{0,5,10,15,20,25,30,3,8,13,18,23,28,1,6,11,16,21,26,31,4,9,14,19,24,29,..., dimensions={0} | all-to-all | bytes 393216 | tf_op jit(solution)/shard_map/all_to_all | solution.py:26
  41.5 0.1 pad_maximum_fusion
  41.6 4.2 %all-gather = f32[64,4,512]{2,1,0:T(4,128)S(1)} all-gather(f32[32,4,512]{2,1,0:T(4,128)S(1)} %pad_maximum_fusion), channel_id=2, replica_groups={{0,32},{64,96},{128,160},{192,224},{256,288},{320,352},{384,416},{448,4..., dimensions={0}, use_global_device_ids=true | all-gather | bytes 786432 | tf_op jit(solution)/shard_map/all_gather | solution.py:183
  45.8 0.0 copy-start.1
  45.8 0.0 copy-done
  45.8 0.0 copy-done.3
  45.8 0.8 shard_map.70
  46.6 12.0 %all_to_all.27.parts_ref = f32[8,128,128]{2,1,0:T(8,128)S(1)} all-to-all(f32[8,128,128]{2,1,0:T(8,128)S(1)} %get-tuple-element.8), channel_id=1, replica_groups={{0,8,16,24,1,9,17,25},{2,10,18,26,3,11,19,27},{4,12,20,28,5,13,21,29},{..., dimensions={0} | all-to-all | bytes 1048576 | tf_op jit(solution)/shard_map/all_to_all | solution.py:26
  58.6 0.0 copy-done.1
  58.6 0.4 shard_map.71
  59.0 13.2 %all_to_all.28.parts_ref = f32[32,4,256]{2,1,0:T(4,128)S(1)} all-to-all(f32[32,4,256]{2,1,0:T(4,128)S(1)} %shard_map.71), channel_id=1, replica_groups={{0,5,10,15,20,25,30,3,8,13,18,23,28,1,6,11,16,21,26,31,4,9,14,19,24,29,..., dimensions={0} | all-to-all | bytes 262144 | tf_op jit(solution)/shard_map/all_to_all | solution.py:26
  72.3 12.5 %all_to_all.29.parts_ref = f32[16,4,128]{2,1,0:T(4,128)S(1)} all-to-all(f32[16,4,128]{2,1,0:T(4,128)S(1)} %get-tuple-element.10), channel_id=1, replica_groups={{0,96,192,288,384,480,64,160,256,352,448,32,128,224,320,416},{1,97,193,..., dimensions={0} | all-to-all | bytes 65536 | tf_op jit(solution)/shard_map/all_to_all | solution.py:26
  84.7 0.6 shard_map.73
  (4 shorter events, 0.1 us)
Async XLA Ops:
  0.6 45.1 %copy-start = (f32[1024,512]{1,0:T(8,128)S(1)}, f32[1024,512]{1,0:T(8,128)}, u32[]{:S(2)}) copy-start(f32[1024,512]{1,0:T(8,128)} %trail_ref.1) | copy-start | bytes 6291460
  1.4 0.7 copy-start.2
  2.2 43.6 %copy-start.3 = (f32[1024,4]{0,1:T(4,128)S(1)}, f32[1024,4]{0,1:T(4,128)}, u32[]{:S(2)}) copy-start(f32[1024,4]{0,1:T(4,128)} %param.7) | copy-start | bytes 49156
  45.8 12.8 %copy-start.1 = (f32[128,128]{1,0:T(8,128)S(1)}, f32[128,128]{1,0:T(8,128)}, u32[]{:S(2)}) copy-start(f32[128,128]{1,0:T(8,128)} %inv_ref.1) | copy-start | bytes 196612

commit v9 on v8

--- a/solution.py
+++ b/solution.py
@@ -19,7 +19,7 @@
 
 def place(col):
     x, y = col // Y_WAYS, col % Y_WAYS
-    return y % BLOCK_Y * BLOCK_X + x % BLOCK_X
+    return (x + y) % BLOCK_Y * BLOCK_X + x % BLOCK_X
 
 
 def exchange(value, axis, groups=None):

time: 85.7 us -> 85.7 us (level)
  no operation moved by 1% of the time
where the time goes in v9:
time: 85.7 us; the launch traced here: 85.3 us
  blocking collectives  81.2 us (95%)
  Pallas kernels  1.9 us (2%)
  between operations  1.48 us (2%)
    all_to_all x5, blocking collectives, exchange(): lax.all_to_all(value, axis, split_axis=0, concat_axis=0, axis_index_group...  77 us
    all_gather x1, blocking collectives, body(): lax.all_gather(jnp.concatenate([got, got[:, :, :128]], axis=2), 'row', ax...  4.19 us

profile of v9, /device:TPU:1, one launch (start us, length us, event | category | flops | bytes accessed | tf_op | source)
XLA Modules:
  0.0 85.3 jit_solution(17050854103780767686)
XLA Ops:
  0.6 0.0 copy-start
  1.4 0.0 copy-start.2
  1.4 0.7 copy-done.2
  2.2 0.0 copy-start.3
  2.2 20.0 %all_to_all.25.every_ref = f32[16,4,512]{2,1,0:T(4,128)S(1)} all-to-all(f32[16,4,512]{2,1,0:T(4,128)S(1)} %shard_map.68), channel_id=1, replica_groups={{0,96,192,288,384,480,64,160,256,352,448,32,128,224,320,416},{1,97,193,..., dimensions={0} | all-to-all | bytes 262144 | tf_op jit(solution)/shard_map/all_to_all | solution.py:26
  22.2 19.3 %all_to_all.26.got_ref = f32[32,4,384]{2,1,0:T(4,128)S(1)} all-to-all(f32[32,4,384]{2,1,0:T(4,128)S(1)} %shard_map.69), channel_id=1, replica_groups={{0,5,10,15,20,25,30,3,8,13,18,23,28,1,6,11,16,21,26,31,4,9,14,19,24,29,..., dimensions={0} | all-to-all | bytes 393216 | tf_op jit(solution)/shard_map/all_to_all | solution.py:26
  41.5 0.1 pad_maximum_fusion
  41.6 4.2 %all-gather = f32[64,4,512]{2,1,0:T(4,128)S(1)} all-gather(f32[32,4,512]{2,1,0:T(4,128)S(1)} %pad_maximum_fusion), channel_id=2, replica_groups={{0,32},{64,96},{128,160},{192,224},{256,288},{320,352},{384,416},{448,4..., dimensions={0}, use_global_device_ids=true | all-gather | bytes 786432 | tf_op jit(solution)/shard_map/all_gather | solution.py:183
  45.8 0.0 copy-start.1
  45.8 0.0 copy-done
  45.8 0.0 copy-done.3
  45.8 0.8 shard_map.70
  46.6 12.0 %all_to_all.27.parts_ref = f32[8,128,128]{2,1,0:T(8,128)S(1)} all-to-all(f32[8,128,128]{2,1,0:T(8,128)S(1)} %get-tuple-element.8), channel_id=1, replica_groups={{0,9,16,25,1,8,17,24},{2,11,18,27,3,10,19,26},{4,13,20,29,5,12,21,28},{..., dimensions={0} | all-to-all | bytes 1048576 | tf_op jit(solution)/shard_map/all_to_all | solution.py:26
  58.6 0.0 copy-done.1
  58.6 0.4 shard_map.71
  59.0 13.2 %all_to_all.28.parts_ref = f32[32,4,256]{2,1,0:T(4,128)S(1)} all-to-all(f32[32,4,256]{2,1,0:T(4,128)S(1)} %shard_map.71), channel_id=1, replica_groups={{0,5,10,15,20,25,30,3,8,13,18,23,28,1,6,11,16,21,26,31,4,9,14,19,24,29,..., dimensions={0} | all-to-all | bytes 262144 | tf_op jit(solution)/shard_map/all_to_all | solution.py:26
  72.3 12.5 %all_to_all.29.parts_ref = f32[16,4,128]{2,1,0:T(4,128)S(1)} all-to-all(f32[16,4,128]{2,1,0:T(4,128)S(1)} %get-tuple-element.10), channel_id=1, replica_groups={{0,96,192,288,384,480,64,160,256,352,448,32,128,224,320,416},{1,97,193,..., dimensions={0} | all-to-all | bytes 65536 | tf_op jit(solution)/shard_map/all_to_all | solution.py:26
  84.7 0.6 shard_map.73
  (4 shorter events, 0.1 us)
Async XLA Ops:
  0.6 45.1 %copy-start = (f32[1024,512]{1,0:T(8,128)S(1)}, f32[1024,512]{1,0:T(8,128)}, u32[]{:S(2)}) copy-start(f32[1024,512]{1,0:T(8,128)} %trail_ref.1) | copy-start | bytes 6291460
  1.4 0.7 copy-start.2
  2.2 43.6 %copy-start.3 = (f32[1024,4]{0,1:T(4,128)S(1)}, f32[1024,4]{0,1:T(4,128)}, u32[]{:S(2)}) copy-start(f32[1024,4]{0,1:T(4,128)} %param.7) | copy-start | bytes 49156
  45.8 12.8 %copy-start.1 = (f32[128,128]{1,0:T(8,128)S(1)}, f32[128,128]{1,0:T(8,128)}, u32[]{:S(2)}) copy-start(f32[128,128]{1,0:T(8,128)} %inv_ref.1) | copy-start | bytes 196612
